TPU v7x, 256 devices: a whole 4x4x8 slice. The times are simulated.
256 devices in a mesh: seq: 32 (over z, y), head: 8 (over x, core).
Axes of the slice: x: 4, y: 4, z: 8, core: 2. Of those that a mesh axis runs over, the one named last changes fastest.
Arguments:
- inputs: bfloat16 [32768, 5120], P('seq', 'head'), may hold values from -0.59765625 to 0.59765625
- gates: bfloat16 [32768, 5120], P('seq', 'head'), may hold values from -6 to 6
- write_keys: bfloat16 [32768, 128], P('seq'), may hold values from -6 to 6
- read_keys: bfloat16 [32768, 128], P('seq'), may hold values from -0.125 to 0.125
- log_decay: float32 [80, 32768], P('head', 'seq'), may hold values from -3 to 0
- skip_gain: float32 [80], P('head'), may hold values from 0.5 to 4
- doc_ids: int32 [32768], P('seq'), may hold values from 0 to 3, never falling along the last dimension, each value on 1 to 16384 neighbouring positions
- out_weight: bfloat16 [5120, 2560], P('head'), may hold values from -0.078125 to 0.078125
- grad_out: bfloat16 [32768, 2560], P(('seq', 'head')), may hold values from -6 to 6
Outputs:
- mixed_out: bfloat16 [32768, 2560], P(('seq', 'head'))
- grad_inputs: bfloat16 [32768, 5120], P('seq', 'head')
Inputs may be any that keep to these rules, and one draw needn't show every extreme that they name: `doc_ids`: document ids never fall along the sequence; every document has 1 to 16384 tokens and one has exactly 16384.
All inputs are finite; a program needn't handle non-finite values.
Results may differ from a plain program's by a relative error of at most 0.02.
Values may be sent and summed in bfloat16 or wider, within the bound.
A program may use at most 128 MiB of HBM per device.

v0:
```python
import jax
import jax.numpy as jnp
from jax import lax
from jax.sharding import Mesh
from jax.sharding import PartitionSpec as P

GROUP = 256
SEQ = ("seq_0", "seq_1")
HEAD = ("head_0", "head_1")
SEQ_HEAD = ("seq_0", "seq_1", "head_0", "head_1")


def passed_along(block, axis, distance):
    devices = range(lax.axis_size(axis))
    route = [(i - distance, i) for i in devices if i - distance in devices]
    return lax.ppermute(block, axis, route)


def joined_along(pieces, dim):
    pieces = jnp.moveaxis(pieces, 0, dim)
    shape = pieces.shape
    return pieces.reshape(*shape[:dim], shape[dim] * shape[dim + 1], *shape[dim + 2 :])


def gather_in_order(shard, axes, sequence):
    pieces = shard[None]
    for k in sequence:
        pieces = lax.all_gather(pieces, axes[k], axis=0, tiled=True)
    current = [lax.axis_size(axes[k]) for k in reversed(sequence)]
    pieces = pieces.reshape(*current, *shard.shape)
    turned = sorted(range(len(sequence)), key=lambda place: sequence[len(sequence) - 1 - place])
    return pieces.transpose(*turned, *range(len(sequence), pieces.ndim)).reshape(-1, *shard.shape)


def whole_of(shard, axes, sequence, dim):
    return joined_along(gather_in_order(shard, axes, sequence), dim)


def nothing_yet(shard, identity):
    return jax.tree.map(
        lambda part, zero: jnp.zeros_like(part) + jnp.asarray(zero, part.dtype), shard, identity
    )


def entering_2(shard, axes, combine, identity, reverse):
    before = start = nothing_yet(shard, identity)
    so_far = shard
    for axis in reversed(axes):
        devices, place = (lax.axis_size(axis), lax.axis_index(axis))
        pieces = jax.tree.map(
            lambda part, kind: lax.all_gather(part.astype(kind), axis),
            so_far,
            (jnp.bfloat16, jnp.bfloat16),
        )
        inside, so_far = (start, start)
        for k in reversed(range(devices)) if reverse else range(devices):
            passed = k > place if reverse else k < place
            so_far = combine(
                so_far, jax.tree.map(lambda part, own: part[k].astype(own.dtype), pieces, shard)
            )
            inside = jax.tree.map(lambda new, old: jnp.where(passed, new, old), so_far, inside)
        before = combine(inside, before)
    return before


def group_terms(write_blk, read_blk, decay_blk, doc_blk, before):
    block_len = doc_blk.shape[0]
    cumul = jnp.cumsum(decay_blk, axis=1)
    positions = jnp.arange(block_len)
    causal_same = (doc_blk[:, None] == doc_blk[None, :]) & (
        positions[:, None] >= positions[None, :]
    )
    spread = jnp.where(causal_same[None], cumul[:, :, None] - cumul[:, None, :], 0.0)
    decay_matrix = jnp.where(causal_same[None], jnp.exp(spread), 0.0)
    scores = jnp.dot(read_blk, write_blk.T, preferred_element_type=jnp.float32)
    weights = (decay_matrix * scores[None]).astype(jnp.bfloat16)
    entry_w = jnp.where((doc_blk == before)[None], jnp.exp(cumul), 0.0)
    exit_w = jnp.where(
        (doc_blk == doc_blk[block_len - 1])[None], jnp.exp(cumul[:, block_len - 1 :] - cumul), 0.0
    )
    return (weights, entry_w, exit_w, entry_w[:, block_len - 1])


def combine(earlier, later):
    return (earlier[0] * later[0], later[0][:, None, None] * earlier[1] + later[1])


def shards(
    inputs, gates, write_keys, read_keys, log_decay, skip_gain, doc_ids, out_weight, grad_out
):
    tok_rows, inner = inputs.shape
    head_count = log_decay.shape[0]
    head_width = inner // head_count
    state_width = write_keys.shape[1]
    group_count = tok_rows // GROUP
    before = passed_along(doc_ids[tok_rows - 1 :] + 1, SEQ, 1) - 1
    doc_blocks = doc_ids.reshape(group_count, GROUP)
    befores = jnp.concatenate([before, doc_blocks[:-1, GROUP - 1]])
    blocks_b = write_keys.reshape(group_count, GROUP, state_width)
    blocks_c = read_keys.reshape(group_count, GROUP, state_width)
    blocks_d = log_decay.reshape(head_count, group_count, GROUP).transpose(1, 0, 2)
    blocks_x = inputs.reshape(group_count, GROUP, head_count, head_width)
    weights, entry_w, exit_w, decays = jax.vmap(group_terms)(
        blocks_b, blocks_c, blocks_d, doc_blocks, befores
    )
    entry_t = jnp.swapaxes(entry_w, 1, 2)[..., None]
    exit_t = jnp.swapaxes(exit_w, 1, 2)[..., None]
    skip_full = skip_gain[:, None]
    inner_mixed = jnp.einsum(
        "khts,kshp->kthp", weights, blocks_x, preferred_element_type=jnp.float32
    )
    write_scaled = (exit_t * blocks_x.astype(jnp.float32)).astype(jnp.bfloat16)
    own_states = jnp.einsum(
        "kshp,ksn->khpn", write_scaled, blocks_b, preferred_element_type=jnp.float32
    )
    empty_state = jnp.zeros((head_count, head_width, state_width), jnp.float32)
    unit_decay = jnp.ones((head_count,), jnp.float32)
    running = empty_state
    run_decay = unit_decay
    enter_states = []
    enter_decays = []
    for position in range(group_count):
        enter_states.append(running)
        enter_decays.append(run_decay)
        running = decays[position][:, None, None] * running + own_states[position]
        run_decay = decays[position] * run_decay
    silu_gate = jax.nn.silu(gates.astype(jnp.float32))
    grad_gated = lax.dot_general(
        whole_of(grad_out, HEAD, (0, 1), 0),
        out_weight,
        (((1,), (1,)), ((), ())),
        preferred_element_type=jnp.float32,
    )
    grad_mix = (grad_gated * silu_gate).astype(jnp.bfloat16)
    blocks_dy = grad_mix.reshape(group_count, GROUP, head_count, head_width)
    inner_grad = jnp.einsum(
        "khts,kthp->kshp", weights, blocks_dy, preferred_element_type=jnp.float32
    )
    grad_scaled = (entry_t * blocks_dy.astype(jnp.float32)).astype(jnp.bfloat16)
    grad_states = jnp.einsum(
        "kthp,ktn->khpn", grad_scaled, blocks_c, preferred_element_type=jnp.float32
    )
    running_back = empty_state
    back_decay = unit_decay
    exit_states = []
    exit_decays = []
    for position in reversed(range(group_count)):
        exit_states.insert(0, running_back)
        exit_decays.insert(0, back_decay)
        running_back = grad_states[position] + decays[position][:, None, None] * running_back
        back_decay = decays[position] * back_decay
    state_in = entering_2((run_decay, running), SEQ, combine, (unit_decay, empty_state), False)[1]
    grad_in = entering_2((run_decay, running_back), SEQ, combine, (unit_decay, empty_state), True)[
        1
    ]
    entering = jnp.stack(
        [
            enter_states[position] + enter_decays[position][:, None, None] * state_in
            for position in range(group_count)
        ]
    ).astype(jnp.bfloat16)
    carried = (
        jnp.einsum("ktn,khpn->kthp", blocks_c, entering, preferred_element_type=jnp.float32)
        * entry_t
    )
    mixed = inner_mixed + carried + skip_full * blocks_x.astype(jnp.float32)
    gated = (mixed.reshape(tok_rows, inner) * silu_gate).astype(jnp.bfloat16)
    mixed_out = lax.psum_scatter(
        jnp.dot(gated, out_weight, preferred_element_type=jnp.float32).astype(jnp.bfloat16),
        HEAD,
        scatter_dimension=0,
        tiled=True,
    )
    arriving = jnp.stack(
        [
            exit_states[position] + exit_decays[position][:, None, None] * grad_in
            for position in range(group_count)
        ]
    ).astype(jnp.bfloat16)
    carried_grad = (
        jnp.einsum("ksn,khpn->kshp", blocks_b, arriving, preferred_element_type=jnp.float32)
        * exit_t
    )
    grad_inputs = (inner_grad + carried_grad + skip_full * blocks_dy.astype(jnp.float32)).astype(
        jnp.bfloat16
    )
    return (mixed_out, grad_inputs.reshape(tok_rows, inner))


def solution(mesh):
    split = Mesh(mesh.devices.reshape(8, 4, 4, 2), ("seq_0", "seq_1", "head_0", "head_1"))
    return jax.shard_map(
        shards,
        mesh=split,
        in_specs=(
            P(SEQ, HEAD),
            P(SEQ, HEAD),
            P(SEQ, None),
            P(SEQ, None),
            P(HEAD, SEQ),
            P(HEAD),
            P(SEQ),
            P(HEAD, None),
            P(SEQ_HEAD, None),
        ),
        out_specs=(P(SEQ_HEAD, None), P(SEQ, HEAD)),
        check_vma=False,
    )
```

profile of v0, /device:TPU:16, one launch (start us, length us, event | category | flops | bytes accessed | tf_op | source)
XLA Modules:
  0.0 246.8 jit_solution(7034171664779118965)
XLA Ops:
  7.2 0.7 all-gather.15.cloned.1.call-update
  8.0 1.5 slice.212
  10.1 4.5 %collective-permute-start = (s32[1]{0:T(128)}, s32[1]{0:T(128)}, u32[]{:S(2)}, u32[]{:S(2)}) collective-permute-start(s32[1]{0:T(128)} %add.280), channel_id=1, source_target_pairs={{0,8},{8,16},{16,24},{24,32},{32,40},{40,48},{48,56},{56,64},{64,7... | collective-permute-start | bytes 20 | tf_op jit(solution)/shard_map/ppermute | solution.py:16
  14.5 0.7 eq.45
  15.2 0.9 reshape.396
  16.2 2.3 reduce-window.6
  19.1 0.4 copy-done.16
  19.6 2.5 %copy.66 = bf16[1024,640]{0,1:T(8,128)(2,1)} copy(bf16[1024,640]{1,0:T(8,128)(2,1)} %param.9) | data formatting | bytes 2621440 | tf_op args[0]
  22.0 0.2 slice_reduce_fusion.5
  23.2 1.5 exponential_select_fusion
  24.7 0.6 copy-done.17
  25.5 3.8 %reshape.401 = bf16[4,256,10,64]{1,0,3,2:T(4,128)(2,1)} reshape(bf16[1024,640]{0,1:T(8,128)(2,1)} %copy.66) | data formatting | bytes 2621440 | tf_op jit(solution)/shard_map/reshape | solution.py:102
  29.3 8.0 %all-gather = bf16[4,10,1]{1,2,0:T(2,128)(2,1)S(1)} all-gather(bf16[1,10,1]{1,2,0:T(2,128)(2,1)S(1)} %copy.68), channel_id=2, replica_groups=mesh['seq_0'=8,'seq_1'=4,'head_0'=4,'head_1'=2] {'seq_1'}, dimensions={0}, use_global_device_ids=true | all-gather | bytes 100 | tf_op jit(solution)/shard_map/all_gather | solution.py:51
  37.3 0.8 copy.71
  38.1 1.1 slice_reduce_fusion.2
  39.3 0.6 fusion.66
  39.8 0.6 broadcast_select_fusion.3
  40.4 0.6 fusion.75
  41.1 1.8 fusion.14
  42.9 1.1 fusion.39
  44.1 13.8 %all_gather.38 = bf16[4,10,64,128]{3,2,1,0:T(8,128)(2,1)S(1)} all-gather(bf16[1,10,64,128]{3,2,1,0:T(8,128)(2,1)S(1)} %get-tuple-element.22), channel_id=1, replica_groups=mesh['seq_0'=8,'seq_1'=4,'head_0'=4,'head_1'=2] {'seq_1'}, dimensions={0}, use_global_device_ids=true | all-gather | bytes 819200 | tf_op jit(solution)/shard_map/all_gather | solution.py:51
  57.9 0.8 copy-done.2
  58.7 0.9 fusion.41
  59.7 0.7 all-gather.11.cloned.1.call-update
  60.5 1.4 copy.64
  61.9 0.6 iota_compare_fusion
  62.5 2.2 fusion.78
  64.7 1.4 copy.73
  66.1 0.5 convert_bitcast_fusion
  66.7 17.7 %all-gather.2 = bf16[8,1,10]{2,1,0:T(2,128)(2,1)S(1)} all-gather(bf16[1,1,10]{2,1,0:T(2,128)(2,1)S(1)} %get-tuple-element.53), channel_id=1, replica_groups=mesh['seq_0'=8,'seq_1'=4,'head_0'=4,'head_1'=2] {'seq_0'}, dimensions={0}, use_global_device_ids=true | all-gather | bytes 180 | tf_op jit(solution)/shard_map/all_gather | solution.py:51
  84.3 0.6 fusion.54
  84.9 0.6 fusion.61
  85.5 15.2 %all-gather.9.cloned.1.call-done = bf16[8,10,64,128]{3,2,1,0:T(8,128)(2,1)} async-done(((bf16[1,10,64,128]{3,2,1,0:T(8,128)(2,1)}), bf16[8,10,64,128]{3,2,1,0:T(8,128)(2,1)}) %all-gather.9.cloned.1.call-update) | async-done | bytes 1310736 | tf_op jit(solution)/shard_map/all_gather | solution.py:51
  100.8 3.4 %fusion.76 = (bf16[1,10,64,128]{3,2,1,0:T(8,128)(2,1)}, f32[1,10,64,128]{3,2,1,0:T(8,128)}) fusion(pred[]{:T(512)S(6)} %gt.39, pred[]{:T(512)S(6)} %gt.38, pred[]{:T(512)S(6)} %gt.37, bf16[4,10,64,128]{3,2,1,0:T(8,128)(2,1)} %copy-done.2, f32[10]{0:T(128)} %copy-done.38, f32[10]{0:T(128)} %copy-done.25, f32[10]{0:T(128)S(1)} %get-tuple-element.55, ...), kind=kLoop, calls=%fused_computation.162 | loop fusion | flops 4014080 | bytes 2458132 | tf_op jit(solution)/shard_map/convert.22
  104.2 17.5 %all-gather.11.cloned.1.call-done = bf16[8,128,2560]{2,1,0:T(8,128)(2,1)} async-done(((bf16[4,128,2560]{2,1,0:T(8,128)(2,1)}), bf16[8,128,2560]{2,1,0:T(8,128)(2,1)}) %all-gather.11.cloned.1.call-update) | async-done | bytes 5242896 | tf_op jit(solution)/shard_map/all_gather | solution.py:28
  121.7 3.1 %copy.76 = bf16[4,2,128,2560]{3,2,1,0:T(8,128)(2,1)S(1)} copy(bf16[4,2,128,2560]{3,2,0,1:T(8,128)(2,1)} %bitcast.206) | data formatting | bytes 10485760 | tf_op jit(solution)/shard_map/transpose | solution.py:32
  124.9 5.4 %multiply_convert_fusion.3 = bf16[1024,640]{1,0:T(8,128)(2,1)} fusion(bf16[1024,2560]{1,0:T(8,128)(2,1)S(1)} %bitcast.207, bf16[640,2560]{1,0:T(8,128)(2,1)S(1)} %copy-done, bf16[1024,640]{1,0:T(8,128)(2,1)S(1)} %copy-done.42), kind=kOutput, calls=%fused_computation.22 | convolution fusion | flops 3360030720 | bytes 11141120 | tf_op jit(solution)/shard_map/dot_general | solution.py:128
  130.3 2.5 %copy.77 = bf16[1024,640]{0,1:T(8,128)(2,1)} copy(bf16[1024,640]{1,0:T(8,128)(2,1)} %multiply_convert_fusion.3) | data formatting | bytes 2621440 | tf_op jit(solution)/shard_map/convert_element_type | solution.py:134
  132.8 3.8 %reshape.404 = bf16[4,256,10,64]{1,0,3,2:T(4,128)(2,1)} reshape(bf16[1024,640]{0,1:T(8,128)(2,1)} %copy.77) | data formatting | bytes 2621440 | tf_op jit(solution)/shard_map/reshape | solution.py:135
  136.7 2.0 fusion.12
  138.8 1.2 add_convert_fusion.5
  140.0 12.0 %all_gather.43 = bf16[4,10,64,128]{3,2,1,0:T(8,128)(2,1)S(1)} all-gather(bf16[1,10,64,128]{3,2,1,0:T(8,128)(2,1)S(1)} %get-tuple-element.58), channel_id=1, replica_groups=mesh['seq_0'=8,'seq_1'=4,'head_0'=4,'head_1'=2] {'seq_1'}, dimensions={0}, use_global_device_ids=true | all-gather | bytes 819200 | tf_op jit(solution)/shard_map/all_gather | solution.py:51
  152.0 0.8 copy-done.1
  152.9 0.9 fusion.40
  153.8 0.2 reduce-scatter.2.cloned.1.call-start
  154.1 1.2 compare_and_fusion
  155.4 1.8 fusion.22
  157.2 4.1 %fusion.3 = f32[4,256,10,64]{1,3,2,0:T(8,128)S(1)} fusion(f32[4,10,64,256]{3,2,1,0:T(8,128)S(1)} %fusion.22, f32[4,256,256]{2,1,0:T(8,128)S(1)} %copy-done.11, f32[4,10,256]{2,1,0:T(8,128)S(1)} %copy-done.22, pred[4,256,256]{2,1,0:T(8,128)(4,1)S(1)} %compare_and_fusion, f32[10]{0:T(128)} %param.14, f32[4,256,10]{1,2,0:T(8,128)S(1)} %copy-done.24, ...), kind=kOutput, calls=%fused_computation.11 | convolution fusion | flops 351928320 | bytes 7946280 | tf_op jit(solution)/shard_map/khts,kshp->kthp/dot_general | solution.py:109
  161.3 1.7 copy.74
  163.0 2.1 copy.84
  165.1 3.3 %copy.75 = f32[1024,640]{1,0:T(8,128)} copy(f32[1024,640]{0,1:T(8,128)} %bitcast.205) | data formatting | bytes 5242880 | tf_op jit(solution)/shard_map/reshape | solution.py:167
  168.3 8.8 %convolution_convert_fusion = bf16[1024,2560]{1,0:T(8,128)(2,1)} fusion(bf16[640,2560]{1,0:T(8,128)(2,1)S(1)} %copy-done, f32[1024,640]{1,0:T(8,128)} %copy.75, bf16[1024,640]{1,0:T(8,128)(2,1)} %param.10), kind=kOutput, calls=%fused_computation.1 | convolution fusion | flops 3362652160 | bytes 12451840 | tf_op jit(solution)/shard_map/dot_general | solution.py:169
  177.2 17.2 %all-gather.3 = bf16[8,1,10]{2,1,0:T(2,128)(2,1)S(1)} all-gather(bf16[1,1,10]{2,1,0:T(2,128)(2,1)} %get-tuple-element.52), channel_id=1, replica_groups=mesh['seq_0'=8,'seq_1'=4,'head_0'=4,'head_1'=2] {'seq_0'}, dimensions={0}, use_global_device_ids=true | all-gather | bytes 180 | tf_op jit(solution)/shard_map/all_gather | solution.py:51
  194.4 0.5 fusion.45
  194.9 0.6 fusion.52
  195.5 0.6 all-gather.13.cloned.1.call-done
  196.1 2.7 %add_convert_fusion.2 = (bf16[1,10,64,128]{3,2,1,0:T(8,128)(2,1)S(1)}, f32[1,10,64,128]{3,2,1,0:T(8,128)S(1)}) fusion(f32[10]{0:T(128)} %get-tuple-element.14, f32[1,10,64,128]{3,2,1,0:T(8,128)} %get-tuple-element.59, f32[10]{0:T(128)S(1)} %get-tuple-element.10, f32[4,10,64,128]{3,2,1,0:T(8,128)} %copy-done.3, pred[]{:T(512)S(6)} %lt.39, pred[]{:T(512)S(6)} %lt.38, ...), kind=kLoop, calls=%fused_computation.61 | loop fusion | flops 4341760 | bytes 3113572 | tf_op jit(solution)/shard_map/convert.18
  198.9 1.3 add_convert_fusion.1
  200.2 0.5 fusion.30
  200.8 3.6 %fusion.9 = bf16[4,256,10,64]{1,3,2,0:T(8,128)(2,1)S(1)} fusion(f32[4,10,64,256]{3,2,1,0:T(8,128)S(1)} %fusion.30, f32[4,256,256]{2,1,0:T(8,128)S(1)} %copy-done.12, f32[4,10,256]{2,1,0:T(8,128)S(1)} %copy-done.23, pred[4,256,256]{2,1,0:T(8,128)(4,1)S(1)} %copy-done.19, f32[10]{0:T(128)S(1)} %copy-done.43, f32[4,256,10]{1,2,0:T(8,128)S(1)} %copy-done.21, ...), kind=kOutput, calls=%fused_computation.17 | convolution fusion | flops 352583680 | bytes 6635560 | tf_op jit(solution)/shard_map/khts,kthp->kshp/dot_general | solution.py:136
  204.4 1.0 copy.80
  205.4 1.4 copy.85
  206.8 2.4 copy.81
  209.2 31.0 %reduce-scatter.2.cloned.1.call-done = bf16[128,2560]{1,0:T(8,128)(2,1)} async-done(((bf16[1024,2560]{1,0:T(8,128)(2,1)}), bf16[128,2560]{1,0:T(8,128)(2,1)}) %reduce-scatter.2.cloned.1.call-update) | async-done | bytes 655376 | tf_op jit(solution)/shard_map/reduce_scatter | solution.py:168
  (111 shorter events, 1.7 us)
Async XLA Ops:
  7.2 117.7 %copy-start = (bf16[640,2560]{1,0:T(8,128)(2,1)S(1)}, bf16[640,2560]{1,0:T(8,128)(2,1)}, u32[]{:S(2)}) copy-start(bf16[640,2560]{1,0:T(8,128)(2,1)} %param.16) | copy-start | bytes 9830404
  7.2 52.6 %all-gather.15.cloned.1.call-start = ((), (), s32[]{:S(2)}) async-start(), calls=%async_computation.5 | async-start | bytes 3276800 | tf_op jit(solution)/shard_map/all_gather | solution.py:28
  7.9 92.9 %all-gather.9.cloned.1.call-start = ((), (), s32[]{:S(2)}) async-start(), calls=%async_computation.1 | async-start | bytes 1474560 | tf_op jit(solution)/shard_map/all_gather | solution.py:51
  10.1 12.3 %collective-permute-start = (s32[1]{0:T(128)}, s32[1]{0:T(128)}, u32[]{:S(2)}, u32[]{:S(2)}) collective-permute-start(s32[1]{0:T(128)} %add.280), channel_id=1, source_target_pairs={{0,8},{8,16},{16,24},{24,32},{32,40},{40,48},{48,56},{56,64},{64,7... | collective-permute-start | bytes 20 | tf_op jit(solution)/shard_map/ppermute | solution.py:16
  18.9 0.6 copy-start.16
  19.6 21.5 %copy-start.14 = (bf16[1024,128]{1,0:T(8,128)(2,1)S(1)}, bf16[1024,128]{1,0:T(8,128)(2,1)}, u32[]{:S(2)}) copy-start(bf16[1024,128]{1,0:T(8,128)(2,1)} %param.11) | copy-start | bytes 786436
  24.7 0.6 copy-start.17
  38.1 19.8 %copy-start.20 = (f32[4,256,10]{1,2,0:T(8,128)}, f32[4,256,10]{1,2,0:T(8,128)S(1)}, u32[]{:S(2)}) copy-start(f32[4,256,10]{1,2,0:T(8,128)S(1)} %copy.71) | copy-start | bytes 122884
  39.2 1.8 copy-start.36
  39.2 18.6 %copy-start.27 = (f32[10]{0:T(128)}, f32[10]{0:T(128)S(1)}, u32[]{:S(2)}) copy-start(f32[10]{0:T(128)S(1)} %get-tuple-element.11) | copy-start | bytes 124
  39.3 18.6 %copy-start.29 = (f32[10]{0:T(128)}, f32[10]{0:T(128)S(1)}, u32[]{:S(2)}) copy-start(f32[10]{0:T(128)S(1)} %get-tuple-element.8) | copy-start | bytes 124
  39.8 18.0 %copy-start.25 = (f32[10]{0:T(128)}, f32[10]{0:T(128)S(1)}, u32[]{:S(2)}) copy-start(f32[10]{0:T(128)S(1)} %get-tuple-element.56) | copy-start | bytes 124
  39.8 18.0 %copy-start.39 = (f32[10]{0:T(128)}, f32[10]{0:T(128)S(1)}, u32[]{:S(2)}) copy-start(f32[10]{0:T(128)S(1)} %get-tuple-element.57) | copy-start | bytes 124
  40.4 17.4 %copy-start.38 = (f32[10]{0:T(128)}, f32[10]{0:T(128)S(1)}, u32[]{:S(2)}) copy-start(f32[10]{0:T(128)S(1)} %get-tuple-element.49) | copy-start | bytes 124
  41.1 16.8 %copy-start.33 = (f32[10]{0:T(128)}, f32[10]{0:T(128)S(1)}, u32[]{:S(2)}) copy-start(f32[10]{0:T(128)S(1)} %get-tuple-element.62) | copy-start | bytes 124
  42.9 1.2 copy-start.4
  44.1 18.4 %copy-start.13 = (bf16[1024,128]{1,0:T(8,128)(2,1)S(1)}, bf16[1024,128]{1,0:T(8,128)(2,1)}, u32[]{:S(2)}) copy-start(bf16[1024,128]{1,0:T(8,128)(2,1)} %param.12) | copy-start | bytes 786436
  57.9 0.8 copy-start.2
  59.7 62.0 %all-gather.11.cloned.1.call-start = ((), (), s32[]{:S(2)}) async-start(), calls=%async_computation.3 | async-start | bytes 7864320 | tf_op jit(solution)/shard_map/all_gather | solution.py:28
  60.4 135.7 %all-gather.13.cloned.1.call-start = ((), (), s32[]{:S(2)}) async-start(), calls=%async_computation.4 | async-start | bytes 1474560 | tf_op jit(solution)/shard_map/all_gather | solution.py:51
  121.7 3.2 %copy-start.42 = (bf16[1024,640]{1,0:T(8,128)(2,1)S(1)}, bf16[1024,640]{1,0:T(8,128)(2,1)}, u32[]{:S(2)}) copy-start(bf16[1024,640]{1,0:T(8,128)(2,1)} %param.10) | copy-start | bytes 3932164
  136.6 2.1 copy-start.5
  136.6 2.1 copy-start.9
  136.6 2.1 copy-start.10
  136.6 2.1 copy-start.30
  136.6 2.1 copy-start.31
  136.6 2.1 copy-start.34
  136.6 2.1 copy-start.37
  136.6 2.1 copy-start.40
  136.7 2.1 copy-start.41
  138.7 1.3 copy-start.3
  138.7 14.2 %copy-start.26 = (f32[10]{0:T(128)S(1)}, f32[10]{0:T(128)}, u32[]{:S(2)}) copy-start(f32[10]{0:T(128)} %copy-done.25) | copy-start | bytes 124
  138.7 14.2 %copy-start.32 = (f32[10]{0:T(128)S(1)}, f32[10]{0:T(128)}, u32[]{:S(2)}) copy-start(f32[10]{0:T(128)} %get-tuple-element.50) | copy-start | bytes 124
  138.7 14.2 %copy-start.35 = (f32[10]{0:T(128)S(1)}, f32[10]{0:T(128)}, u32[]{:S(2)}) copy-start(f32[10]{0:T(128)} %get-tuple-element.54) | copy-start | bytes 124
  152.0 0.8 copy-start.1
  153.8 86.4 %reduce-scatter.2.cloned.1.call-start = ((), (), s32[]{:S(2)}) async-start(), calls=%async_computation.2 | async-start | bytes 5898240 | tf_op jit(solution)/shard_map/reduce_scatter | solution.py:168
  154.1 3.1 %copy-start.7 = (bf16[4,256,10,64]{1,0,3,2:T(4,128)(2,1)S(1)}, bf16[4,256,10,64]{1,0,3,2:T(4,128)(2,1)}, u32[]{:S(2)}) copy-start(bf16[4,256,10,64]{1,0,3,2:T(4,128)(2,1)} %reshape.401) | copy-start | bytes 3932164
  154.1 3.1 %copy-start.11 = (f32[4,256,256]{2,1,0:T(8,128)S(1)}, f32[4,256,256]{2,1,0:T(8,128)}, u32[]{:S(2)}) copy-start(f32[4,256,256]{2,1,0:T(8,128)} %fusion.78) | copy-start | bytes 3145732
  154.1 3.1 %copy-start.22 = (f32[4,10,256]{2,1,0:T(8,128)S(1)}, f32[4,10,256]{2,1,0:T(8,128)}, u32[]{:S(2)}) copy-start(f32[4,10,256]{2,1,0:T(8,128)} %copy.64) | copy-start | bytes 122884
  154.1 3.1 %copy-start.24 = (f32[4,256,10]{1,2,0:T(8,128)S(1)}, f32[4,256,10]{1,2,0:T(8,128)}, u32[]{:S(2)}) copy-start(f32[4,256,10]{1,2,0:T(8,128)} %copy.73) | copy-start | bytes 122884
  155.4 5.9 %copy-start.18 = (pred[4,256,256]{2,1,0:T(8,128)(4,1)}, pred[4,256,256]{2,1,0:T(8,128)(4,1)S(1)}, u32[]{:S(2)}) copy-start(pred[4,256,256]{2,1,0:T(8,128)(4,1)S(1)} %compare_and_fusion) | copy-start | bytes 786436
  177.1 21.7 %copy-start.28 = (f32[10]{0:T(128)S(1)}, f32[10]{0:T(128)}, u32[]{:S(2)}) copy-start(f32[10]{0:T(128)} %copy-done.27) | copy-start | bytes 124
  177.2 23.0 %copy-start.15 = (bf16[1024,128]{1,0:T(8,128)(2,1)S(1)}, bf16[1024,128]{1,0:T(8,128)(2,1)}, u32[]{:S(2)}) copy-start(bf16[1024,128]{1,0:T(8,128)(2,1)} %param.11) | copy-start | bytes 786436
  196.1 2.8 %copy-start.6 = (f32[1,10,64,128]{3,2,1,0:T(8,128)S(1)}, f32[1,10,64,128]{3,2,1,0:T(8,128)}, u32[]{:S(2)}) copy-start(f32[1,10,64,128]{3,2,1,0:T(8,128)} %get-tuple-element.59) | copy-start | bytes 983044
  198.8 1.9 copy-start.8
  198.8 1.9 copy-start.12
  198.8 1.9 copy-start.19
  198.8 1.9 copy-start.21
  198.8 1.9 copy-start.23
  198.9 1.9 copy-start.43
Sparse Core Ops, SparseCore 0:
  9.8 40.5 all-gather.14
  59.8 40.9 all-gather.8
  102.6 19.0 all-gather.10
  154.0 42.0 all-gather.12
  199.0 41.1 reduce-scatter.1
where the time goes:
time: 248 us; the launch traced here: 247 us
  blocking collectives  68.6 us (28%)
  waiting for transfers between devices  65.7 us (26%)
  local copies, waits for them, and re-layouts  39.3 us (16%)
  matrix products  30.2 us (12%)
  other arithmetic  22.3 us (9%)
  between operations  15.8 us (6%)
  starting transfers between devices  4.85 us (2%)
    all_gather x5, blocking collectives, entering_2(): lax.all_gather(part.astype(kind), axis)  68.6 us
    reduce_scatter x1, waiting for transfers between devices, shards(): lax.psum_scatter(jnp.dot(gated, out_weight, preferred_element_type=jnp.fl...  31 us
    all_gather x2, waiting for transfers between devices, gather_in_order(): pieces = lax.all_gather(pieces, axes[k], axis=0, tiled=True)  17.5 us
    all_gather x2, waiting for transfers between devices, entering_2(): lax.all_gather(part.astype(kind), axis)  15.8 us
    unnamed x92, local copies, waits for them, and re-layouts  11.3 us
    another operation x7, other arithmetic  11.1 us
    dot_general x1, matrix products, shards(): jnp.dot(gated, out_weight, preferred_element_type=jnp.float32)  8.8 us
    dot_general x1, matrix products, shards(): lax.dot_general(whole_of(grad_out, HEAD, (0, 1), 0), out_weight, (((1,),...  5.44 us
  transfers between devices with their start and end apart: 6, of which 4 were waited for; matrix products, arithmetic and copies ran while one was open for 28% of the time, Pallas kernels for 0%

commit v1 on v0

--- a/solution.py
+++ b/solution.py
@@ -25,7 +25,9 @@
 def gather_in_order(shard, axes, sequence):
     pieces = shard[None]
     for k in sequence:
-        pieces = lax.all_gather(pieces, axes[k], axis=0, tiled=True)
+        pieces = jnp.concatenate(
+            lax.all_to_all(jnp.stack([pieces] * lax.axis_size(axes[k])), axes[k], 0, 0), axis=0
+        )
     current = [lax.axis_size(axes[k]) for k in reversed(sequence)]
     pieces = pieces.reshape(*current, *shard.shape)
     turned = sorted(range(len(sequence)), key=lambda place: sequence[len(sequence) - 1 - place])

time: 248 us -> 230 us (0.927)
  waiting for transfers between devices: 65.7 us -> 32 us
  blocking collectives: 68.6 us -> 75.1 us
  starting transfers between devices: 4.85 us -> 9.47 us
  other arithmetic: 22.3 us -> 26.9 us
    all_gather x2 -> x0, waiting for transfers between devices: 17.5 us -> none  [gather_in_order(): pieces = lax.all_gather(pieces, axes[k], axis=0, tiled=True)]
    all_gather x2, waiting for transfers between devices: 15.8 us -> 0.74 us  [entering_2(): lax.all_gather(part.astype(kind), axis)]
    all_to_all x0 -> x1, blocking collectives: none -> 7.95 us  [gather_in_order(): lax.all_to_all(jnp.stack([pieces] * lax.axis_size(axes[k])), axes[k], 0, 0)]
    all_to_all x0 -> x1, starting transfers between devices: none -> 4.69 us  [gather_in_order(): lax.all_to_all(jnp.stack([pieces] * lax.axis_size(axes[k])), axes[k], 0, 0)]
    another operation x7 -> x8, other arithmetic: 11.1 us -> 15 us
    transpose x1 -> x0, local copies, waits for them, and re-layouts: 3.14 us -> none  [gather_in_order(): pieces.transpose(*turned, *range(len(sequence), pieces.ndim))]
    unnamed x92 -> x78, local copies, waits for them, and re-layouts: 11.3 us -> 11.8 us
  transfers between devices with their start and end apart: 6 -> 5, of which waited for: 4 -> 2; matrix products, arithmetic and copies ran while one was open for 28% -> 37% of each run, Pallas kernels for 0% -> 0%
where the time goes in v1:
time: 230 us; the launch traced here: 228 us
  blocking collectives  75.1 us (33%)
  local copies, waits for them, and re-layouts  38 us (17%)
  waiting for transfers between devices  32 us (14%)
  matrix products  31.3 us (14%)
  other arithmetic  26.9 us (12%)
  between operations  15.6 us (7%)
  starting transfers between devices  9.47 us (4%)
    all_gather x5, blocking collectives, entering_2(): lax.all_gather(part.astype(kind), axis)  67.1 us
    reduce_scatter x1, waiting for transfers between devices, shards(): lax.psum_scatter(jnp.dot(gated, out_weight, preferred_element_type=jnp.fl...  31.2 us
    another operation x7, other arithmetic  12 us
    unnamed x78, local copies, waits for them, and re-layouts  11.8 us
    dot_general x1, matrix products, shards(): jnp.dot(gated, out_weight, preferred_element_type=jnp.float32)  8.78 us
    all_to_all x1, blocking collectives, gather_in_order(): lax.all_to_all(jnp.stack([pieces] * lax.axis_size(axes[k])), axes[k], 0, 0)  7.95 us
    dot_general x1, matrix products, shards(): lax.dot_general(whole_of(grad_out, HEAD, (0, 1), 0), out_weight, (((1,),...  5.46 us
    all_to_all x1, starting transfers between devices, gather_in_order(): lax.all_to_all(jnp.stack([pieces] * lax.axis_size(axes[k])), axes[k], 0, 0)  4.69 us
  transfers between devices with their start and end apart: 5, of which 2 were waited for; matrix products, arithmetic and copies ran while one was open for 37% of the time, Pallas kernels for 0%

profile of v1, /device:TPU:16, one launch (start us, length us, event | category | flops | bytes accessed | tf_op | source)
XLA Modules:
  0.0 228.4 jit_solution(16081189033949292778)
XLA Ops:
  7.2 1.4 slice.212
  9.3 4.5 %collective-permute-start = (s32[1]{0:T(128)}, s32[1]{0:T(128)}, u32[]{:S(2)}, u32[]{:S(2)}) collective-permute-start(s32[1]{0:T(128)} %add.280), channel_id=1, source_target_pairs={{0,8},{8,16},{16,24},{24,32},{32,40},{40,48},{48,56},{56,64},{64,7... | collective-permute-start | bytes 20 | tf_op jit(solution)/shard_map/ppermute | solution.py:16
  13.7 2.8 %stack.11 = bf16[4,1,128,2560]{3,2,1,0:T(8,128)(2,1)} broadcast(bf16[128,2560]{1,0:T(8,128)(2,1)} %param.17), dimensions={2,3} | broadcast | bytes 3276800 | tf_op jit(solution)/shard_map/stack | solution.py:29
  16.6 4.7 %all-to-all-start = ((bf16[4,1,128,2560]{3,2,1,0:T(8,128)(2,1)}), bf16[4,1,128,2560]{3,2,1,0:T(8,128)(2,1)}, u32[]{:S(2)}, u32[]{:S(2)}) async-start(bf16[4,1,128,2560]{3,2,1,0:T(8,128)(2,1)} %stack.11), calls=%async_computation.1 | async-start | bytes 5242880 | tf_op jit(solution)/shard_map/all_to_all | solution.py:29
  21.3 0.7 slice_reduce_fusion.5
  22.0 0.2 slice_reduce_fusion.4
  22.3 2.3 %reduce-window.6 = f32[4,10,2,128]{3,1,2,0:T(8,128)S(1)} reduce-window(f32[4,10,2,128]{3,1,2,0:T(8,128)S(1)} %copy.59, f32[]{:T(128)} %constant.15.clone.1), window={size=1x1x1x128 pad=0_0x0_0x0_0x127_0}, to_apply=%region_0.0 | reduce-window | flops 1300480 | bytes 81924 | tf_op jit(solution)/shard_map/reduce-window
  25.1 0.6 copy.63
  25.8 0.7 iota_compare_fusion
  26.6 2.5 %copy.65 = bf16[1024,640]{0,1:T(8,128)(2,1)} copy(bf16[1024,640]{1,0:T(8,128)(2,1)} %param.9) | data formatting | bytes 2621440 | tf_op args[0]
  29.1 3.8 %reshape.400 = bf16[4,256,10,64]{1,0,3,2:T(4,128)(2,1)} reshape(bf16[1024,640]{0,1:T(8,128)(2,1)} %copy.65) | data formatting | bytes 2621440 | tf_op jit(solution)/shard_map/reshape | solution.py:104
  32.9 2.3 fusion.78
  35.8 0.7 pad_add_fusion
  36.5 1.5 exponential_select_fusion
  38.0 0.6 copy-done.14
  38.8 7.9 %all-gather = bf16[4,10,1]{1,2,0:T(2,128)(2,1)S(1)} all-gather(bf16[1,10,1]{1,2,0:T(2,128)(2,1)S(1)} %copy.67), channel_id=2, replica_groups=mesh['seq_0'=8,'seq_1'=4,'head_0'=4,'head_1'=2] {'seq_1'}, dimensions={0}, use_global_device_ids=true | all-gather | bytes 100 | tf_op jit(solution)/shard_map/all_gather | solution.py:53
  46.8 0.6 fusion.66
  47.3 0.6 broadcast_select_fusion.3
  47.9 1.2 slice_reduce_fusion.2
  49.1 0.8 copy.70
  50.0 0.6 fusion.75
  50.6 1.8 fusion.14
  52.5 1.1 fusion.39
  53.6 13.6 %all_gather.32 = bf16[4,10,64,128]{3,2,1,0:T(8,128)(2,1)S(1)} all-gather(bf16[1,10,64,128]{3,2,1,0:T(8,128)(2,1)S(1)} %get-tuple-element.22), channel_id=1, replica_groups=mesh['seq_0'=8,'seq_1'=4,'head_0'=4,'head_1'=2] {'seq_1'}, dimensions={0}, use_global_device_ids=true | all-gather | bytes 819200 | tf_op jit(solution)/shard_map/all_gather | solution.py:53
  67.3 0.8 copy-done.2
  68.1 0.9 fusion.41
  69.1 1.4 copy.72
  70.5 0.6 convert_bitcast_fusion
  71.1 17.7 %all-gather.1 = bf16[8,1,10]{2,1,0:T(2,128)(2,1)S(1)} all-gather(bf16[1,1,10]{2,1,0:T(2,128)(2,1)S(1)} %get-tuple-element.53), channel_id=1, replica_groups=mesh['seq_0'=8,'seq_1'=4,'head_0'=4,'head_1'=2] {'seq_0'}, dimensions={0}, use_global_device_ids=true | all-gather | bytes 180 | tf_op jit(solution)/shard_map/all_gather | solution.py:53
  88.8 0.6 fusion.54
  89.4 0.5 fusion.61
  90.0 3.0 %pad_maximum_fusion = bf16[2,4,128,2560]{3,2,1,0:T(8,128)(2,1)S(1)} fusion(bf16[1,4,128,2560]{3,2,1,0:T(8,128)(2,1)} %bitcast.30), kind=kLoop, calls=%fused_computation.2 | loop fusion | flops 2621440 | bytes 7864320 | tf_op jit(solution)/shard_map/stack | solution.py:29
  93.0 7.9 %all_to_all.10 = bf16[2,4,128,2560]{3,2,1,0:T(8,128)(2,1)S(1)} all-to-all(bf16[2,4,128,2560]{3,2,1,0:T(8,128)(2,1)S(1)} %pad_maximum_fusion), channel_id=1, replica_groups=mesh['seq_0'=8,'seq_1'=4,'head_0'=4,'head_1'=2] {'head_1'}, dimensions={0} | all-to-all | bytes 10485760 | tf_op jit(solution)/shard_map/all_to_all | solution.py:29
  101.0 0.3 copy.75
  101.3 1.0 copy-done.35
  102.3 5.5 %multiply_convert_fusion.3 = bf16[1024,640]{1,0:T(8,128)(2,1)} fusion(bf16[1024,2560]{1,0:T(8,128)(2,1)S(1)} %bitcast.205, bf16[640,2560]{1,0:T(8,128)(2,1)S(1)} %copy-done, bf16[1024,640]{1,0:T(8,128)(2,1)S(1)} %copy-done.35), kind=kOutput, calls=%fused_computation.23 | convolution fusion | flops 3360030720 | bytes 11141120 | tf_op jit(solution)/shard_map/dot_general | solution.py:130
  107.7 2.5 %copy.76 = bf16[1024,640]{0,1:T(8,128)(2,1)} copy(bf16[1024,640]{1,0:T(8,128)(2,1)} %multiply_convert_fusion.3) | data formatting | bytes 2621440 | tf_op jit(solution)/shard_map/convert_element_type | solution.py:136
  110.2 3.8 %reshape.402 = bf16[4,256,10,64]{1,0,3,2:T(4,128)(2,1)} reshape(bf16[1024,640]{0,1:T(8,128)(2,1)} %copy.76) | data formatting | bytes 2621440 | tf_op jit(solution)/shard_map/reshape | solution.py:137
  114.0 3.0 %fusion.12 = f32[4,10,64,128]{3,2,1,0:T(8,128)} fusion(bf16[4,256,128,1]{2,1,3,0:T(8,128)(2,1)S(1)} %bitcast.209, f32[4,256,10]{1,2,0:T(8,128)} %copy.72, bf16[4,256,10,64]{1,0,3,2:T(4,128)(2,1)} %reshape.402), kind=kOutput, calls=%fused_computation.25 | convolution fusion | flops 169738240 | bytes 2924544 | tf_op jit(solution)/shard_map/kthp,ktn->khpn/dot_general | solution.py:142
  116.9 3.4 %fusion.76 = (bf16[1,10,64,128]{3,2,1,0:T(8,128)(2,1)}, f32[1,10,64,128]{3,2,1,0:T(8,128)S(1)}) fusion(pred[]{:T(512)S(6)} %gt.39, pred[]{:T(512)S(6)} %gt.38, pred[]{:T(512)S(6)} %gt.37, bf16[4,10,64,128]{3,2,1,0:T(8,128)(2,1)} %copy-done.2, f32[10]{0:T(128)} %copy-done.32, f32[10]{0:T(128)S(1)} %copy-done.24, f32[10]{0:T(128)S(1)} %get-tuple-element.55, ...), kind=kLoop, calls=%fused_computation.163 | loop fusion | flops 4014080 | bytes 2458132 | tf_op jit(solution)/shard_map/convert.22
  120.3 2.2 add_convert_fusion.5
  122.5 13.4 %all_gather.35 = bf16[4,10,64,128]{3,2,1,0:T(8,128)(2,1)S(1)} all-gather(bf16[1,10,64,128]{3,2,1,0:T(8,128)(2,1)S(1)} %get-tuple-element.58), channel_id=1, replica_groups=mesh['seq_0'=8,'seq_1'=4,'head_0'=4,'head_1'=2] {'seq_1'}, dimensions={0}, use_global_device_ids=true | all-gather | bytes 819200 | tf_op jit(solution)/shard_map/all_gather | solution.py:53
  136.0 0.8 copy-done.1
  136.8 0.9 fusion.40
  137.8 0.2 reduce-scatter.2.cloned.1.call-start
  138.0 1.2 compare_and_fusion
  139.3 1.8 fusion.22
  141.1 4.1 %fusion.3 = f32[4,256,10,64]{1,3,2,0:T(8,128)S(1)} fusion(f32[4,10,64,256]{3,2,1,0:T(8,128)S(1)} %fusion.22, f32[4,256,256]{2,1,0:T(8,128)S(1)} %copy-done.9, f32[4,10,256]{2,1,0:T(8,128)S(1)} %copy-done.18, pred[4,256,256]{2,1,0:T(8,128)(4,1)S(1)} %compare_and_fusion, f32[10]{0:T(128)} %param.14, f32[4,256,10]{1,2,0:T(8,128)S(1)} %copy-done.22, ...), kind=kOutput, calls=%fused_computation.12 | convolution fusion | flops 351928320 | bytes 7946280 | tf_op jit(solution)/shard_map/khts,kshp->kthp/dot_general | solution.py:111
  145.2 1.7 copy.73
  146.9 2.1 copy.83
  149.0 3.3 %copy.74 = f32[1024,640]{1,0:T(8,128)} copy(f32[1024,640]{0,1:T(8,128)} %bitcast.204) | data formatting | bytes 5242880 | tf_op jit(solution)/shard_map/reshape | solution.py:169
  152.2 8.8 %convolution_convert_fusion = bf16[1024,2560]{1,0:T(8,128)(2,1)} fusion(bf16[640,2560]{1,0:T(8,128)(2,1)S(1)} %copy-done, f32[1024,640]{1,0:T(8,128)} %copy.74, bf16[1024,640]{1,0:T(8,128)(2,1)} %param.10), kind=kOutput, calls=%fused_computation.1 | convolution fusion | flops 3362652160 | bytes 12451840 | tf_op jit(solution)/shard_map/dot_general | solution.py:171
  161.1 14.4 %all-gather.2 = bf16[8,1,10]{2,1,0:T(2,128)(2,1)S(1)} all-gather(bf16[1,1,10]{2,1,0:T(2,128)(2,1)} %get-tuple-element.52), channel_id=1, replica_groups=mesh['seq_0'=8,'seq_1'=4,'head_0'=4,'head_1'=2] {'seq_0'}, dimensions={0}, use_global_device_ids=true | all-gather | bytes 180 | tf_op jit(solution)/shard_map/all_gather | solution.py:53
  175.5 0.6 fusion.45
  176.1 0.6 fusion.52
  176.8 0.7 all-gather.8.cloned.1.call-done
  177.5 2.7 %add_convert_fusion.2 = (bf16[1,10,64,128]{3,2,1,0:T(8,128)(2,1)S(1)}, f32[1,10,64,128]{3,2,1,0:T(8,128)S(1)}) fusion(f32[10]{0:T(128)} %get-tuple-element.14, f32[1,10,64,128]{3,2,1,0:T(8,128)} %get-tuple-element.59, f32[10]{0:T(128)S(1)} %get-tuple-element.10, f32[4,10,64,128]{3,2,1,0:T(8,128)} %fusion.12, pred[]{:T(512)S(6)} %lt.39, pred[]{:T(512)S(6)} %lt.38, ...), kind=kLoop, calls=%fused_computation.62 | loop fusion | flops 4341760 | bytes 3113572 | tf_op jit(solution)/shard_map/convert.18
  180.3 1.3 add_convert_fusion.1
  181.6 0.5 fusion.30
  182.2 3.6 %fusion.9 = bf16[4,256,10,64]{1,3,2,0:T(8,128)(2,1)S(1)} fusion(f32[4,10,64,256]{3,2,1,0:T(8,128)S(1)} %fusion.30, f32[4,256,256]{2,1,0:T(8,128)S(1)} %copy-done.10, f32[4,10,256]{2,1,0:T(8,128)S(1)} %copy-done.19, pred[4,256,256]{2,1,0:T(8,128)(4,1)S(1)} %copy-done.16, f32[10]{0:T(128)S(1)} %copy-done.36, f32[4,256,10]{1,2,0:T(8,128)S(1)} %copy-done.21, ...), kind=kOutput, calls=%fused_computation.18 | convolution fusion | flops 352583680 | bytes 6635560 | tf_op jit(solution)/shard_map/khts,kthp->kshp/dot_general | solution.py:138
  185.8 1.0 copy.79
  186.9 1.3 copy.84
  188.2 2.4 %copy.80 = bf16[1024,640]{1,0:T(8,128)(2,1)} copy(bf16[1024,640]{0,1:T(8,128)(2,1)} %bitcast.207) | data formatting | bytes 2621440
  190.6 31.2 %reduce-scatter.2.cloned.1.call-done = bf16[128,2560]{1,0:T(8,128)(2,1)} async-done(((bf16[1024,2560]{1,0:T(8,128)(2,1)}), bf16[128,2560]{1,0:T(8,128)(2,1)}) %reduce-scatter.2.cloned.1.call-update) | async-done | bytes 655376 | tf_op jit(solution)/shard_map/reduce_scatter | solution.py:170
  (96 shorter events, 1.4 us)
Async XLA Ops:
  7.2 94.1 %copy-start = (bf16[640,2560]{1,0:T(8,128)(2,1)S(1)}, bf16[640,2560]{1,0:T(8,128)(2,1)}, u32[]{:S(2)}) copy-start(bf16[640,2560]{1,0:T(8,128)(2,1)} %param.16) | copy-start | bytes 9830404
  9.3 25.9 %collective-permute-start = (s32[1]{0:T(128)}, s32[1]{0:T(128)}, u32[]{:S(2)}, u32[]{:S(2)}) collective-permute-start(s32[1]{0:T(128)} %add.280), channel_id=1, source_target_pairs={{0,8},{8,16},{16,24},{24,32},{32,40},{40,48},{48,56},{56,64},{64,7... | collective-permute-start | bytes 20 | tf_op jit(solution)/shard_map/ppermute | solution.py:16
  16.6 4.8 %copy-start.34 = (s32[1024]{0:T(1024)S(1)}, s32[1024]{0:T(1024)}, u32[]{:S(2)}) copy-start(s32[1024]{0:T(1024)} %param.15) | copy-start | bytes 12292
  16.6 5.7 %copy-start.17 = (f32[10,1024]{1,0:T(8,128)S(1)}, f32[10,1024]{1,0:T(8,128)}, u32[]{:S(2)}) copy-start(f32[10,1024]{1,0:T(8,128)} %param.13) | copy-start | bytes 122884
  16.6 73.4 %all-to-all-start = ((bf16[4,1,128,2560]{3,2,1,0:T(8,128)(2,1)}), bf16[4,1,128,2560]{3,2,1,0:T(8,128)(2,1)}, u32[]{:S(2)}, u32[]{:S(2)}) async-start(bf16[4,1,128,2560]{3,2,1,0:T(8,128)(2,1)} %stack.11), calls=%async_computation.1 | async-start | bytes 5242880 | tf_op jit(solution)/shard_map/all_to_all | solution.py:29
  21.3 95.7 %all-gather.6.cloned.1.call-start = ((), (), s32[]{:S(2)}) async-start(), calls=%async_computation.3 | async-start | bytes 1474560 | tf_op jit(solution)/shard_map/all_gather | solution.py:53
  25.0 1.5 copy-start.13
  26.6 6.2 %copy-start.11 = (bf16[1024,128]{1,0:T(8,128)(2,1)S(1)}, bf16[1024,128]{1,0:T(8,128)(2,1)}, u32[]{:S(2)}) copy-start(bf16[1024,128]{1,0:T(8,128)(2,1)} %param.12) | copy-start | bytes 786436
  38.0 0.6 copy-start.14
  47.3 20.0 %copy-start.23 = (f32[10]{0:T(128)}, f32[10]{0:T(128)S(1)}, u32[]{:S(2)}) copy-start(f32[10]{0:T(128)S(1)} %get-tuple-element.56) | copy-start | bytes 124
  47.3 20.0 %copy-start.33 = (f32[10]{0:T(128)}, f32[10]{0:T(128)S(1)}, u32[]{:S(2)}) copy-start(f32[10]{0:T(128)S(1)} %get-tuple-element.57) | copy-start | bytes 124
  47.9 19.4 %copy-start.32 = (f32[10]{0:T(128)}, f32[10]{0:T(128)S(1)}, u32[]{:S(2)}) copy-start(f32[10]{0:T(128)S(1)} %get-tuple-element.49) | copy-start | bytes 124
  49.1 1.5 copy-start.31
  49.1 18.1 %copy-start.25 = (f32[10]{0:T(128)}, f32[10]{0:T(128)S(1)}, u32[]{:S(2)}) copy-start(f32[10]{0:T(128)S(1)} %get-tuple-element.11) | copy-start | bytes 124
  49.1 18.1 %copy-start.27 = (f32[10]{0:T(128)}, f32[10]{0:T(128)S(1)}, u32[]{:S(2)}) copy-start(f32[10]{0:T(128)S(1)} %get-tuple-element.8) | copy-start | bytes 124
  49.9 17.3 %copy-start.20 = (f32[4,256,10]{1,2,0:T(8,128)}, f32[4,256,10]{1,2,0:T(8,128)S(1)}, u32[]{:S(2)}) copy-start(f32[4,256,10]{1,2,0:T(8,128)S(1)} %copy.70) | copy-start | bytes 122884
  50.6 16.7 %copy-start.29 = (f32[10]{0:T(128)}, f32[10]{0:T(128)S(1)}, u32[]{:S(2)}) copy-start(f32[10]{0:T(128)S(1)} %get-tuple-element.62) | copy-start | bytes 124
  52.4 1.2 copy-start.4
  67.3 0.8 copy-start.2
  69.1 108.4 %all-gather.8.cloned.1.call-start = ((), (), s32[]{:S(2)}) async-start(), calls=%async_computation.5 | async-start | bytes 1474560 | tf_op jit(solution)/shard_map/all_gather | solution.py:53
  100.9 1.3 copy-start.35
  110.2 6.7 %copy-start.24 = (f32[10]{0:T(128)S(1)}, f32[10]{0:T(128)}, u32[]{:S(2)}) copy-start(f32[10]{0:T(128)} %copy-done.23) | copy-start | bytes 124
  116.9 3.4 %copy-start.3 = (f32[4,10,64,128]{3,2,1,0:T(8,128)S(1)}, f32[4,10,64,128]{3,2,1,0:T(8,128)}, u32[]{:S(2)}) copy-start(f32[4,10,64,128]{3,2,1,0:T(8,128)} %fusion.12) | copy-start | bytes 3932164
  116.9 3.4 %copy-start.8 = (f32[1,10,64,128]{3,2,1,0:T(8,128)S(1)}, f32[1,10,64,128]{3,2,1,0:T(8,128)}, u32[]{:S(2)}) copy-start(f32[1,10,64,128]{3,2,1,0:T(8,128)} %get-tuple-element.23) | copy-start | bytes 983044
  120.3 16.5 %copy-start.28 = (f32[10]{0:T(128)S(1)}, f32[10]{0:T(128)}, u32[]{:S(2)}) copy-start(f32[10]{0:T(128)} %get-tuple-element.50) | copy-start | bytes 124
  120.3 16.5 %copy-start.30 = (f32[10]{0:T(128)S(1)}, f32[10]{0:T(128)}, u32[]{:S(2)}) copy-start(f32[10]{0:T(128)} %get-tuple-element.54) | copy-start | bytes 124
  136.0 0.8 copy-start.1
  137.8 84.1 %reduce-scatter.2.cloned.1.call-start = ((), (), s32[]{:S(2)}) async-start(), calls=%async_computation.4 | async-start | bytes 5898240 | tf_op jit(solution)/shard_map/reduce_scatter | solution.py:170
  138.0 3.1 %copy-start.6 = (bf16[4,256,10,64]{1,0,3,2:T(4,128)(2,1)S(1)}, bf16[4,256,10,64]{1,0,3,2:T(4,128)(2,1)}, u32[]{:S(2)}) copy-start(bf16[4,256,10,64]{1,0,3,2:T(4,128)(2,1)} %reshape.400) | copy-start | bytes 3932164
  138.0 3.1 %copy-start.9 = (f32[4,256,256]{2,1,0:T(8,128)S(1)}, f32[4,256,256]{2,1,0:T(8,128)}, u32[]{:S(2)}) copy-start(f32[4,256,256]{2,1,0:T(8,128)} %fusion.78) | copy-start | bytes 3145732
  138.0 3.1 %copy-start.18 = (f32[4,10,256]{2,1,0:T(8,128)S(1)}, f32[4,10,256]{2,1,0:T(8,128)}, u32[]{:S(2)}) copy-start(f32[4,10,256]{2,1,0:T(8,128)} %copy.63) | copy-start | bytes 122884
  138.0 3.1 %copy-start.22 = (f32[4,256,10]{1,2,0:T(8,128)S(1)}, f32[4,256,10]{1,2,0:T(8,128)}, u32[]{:S(2)}) copy-start(f32[4,256,10]{1,2,0:T(8,128)} %copy.72) | copy-start | bytes 122884
  139.3 5.9 %copy-start.15 = (pred[4,256,256]{2,1,0:T(8,128)(4,1)}, pred[4,256,256]{2,1,0:T(8,128)(4,1)S(1)}, u32[]{:S(2)}) copy-start(pred[4,256,256]{2,1,0:T(8,128)(4,1)S(1)} %compare_and_fusion) | copy-start | bytes 786436
  161.1 19.3 %copy-start.26 = (f32[10]{0:T(128)S(1)}, f32[10]{0:T(128)}, u32[]{:S(2)}) copy-start(f32[10]{0:T(128)} %copy-done.25) | copy-start | bytes 124
  161.1 20.6 %copy-start.12 = (bf16[1024,128]{1,0:T(8,128)(2,1)S(1)}, bf16[1024,128]{1,0:T(8,128)(2,1)}, u32[]{:S(2)}) copy-start(bf16[1024,128]{1,0:T(8,128)(2,1)} %param.11) | copy-start | bytes 786436
  177.5 2.8 %copy-start.5 = (f32[1,10,64,128]{3,2,1,0:T(8,128)S(1)}, f32[1,10,64,128]{3,2,1,0:T(8,128)}, u32[]{:S(2)}) copy-start(f32[1,10,64,128]{3,2,1,0:T(8,128)} %get-tuple-element.59) | copy-start | bytes 983044
  180.2 1.9 copy-start.7
  180.2 1.9 copy-start.10
  180.3 1.9 copy-start.16
  180.3 1.9 copy-start.19
  180.3 1.9 copy-start.21
  180.3 1.9 copy-start.36
Sparse Core Ops, SparseCore 0:
  69.2 41.3 all-gather.5
  137.9 39.5 all-gather.7
  180.6 41.1 reduce-scatter.1
